TPU v7x, 32 devices: a whole 2x2x4 slice. The times are simulated.
32 devices in a mesh: grp: 2 (over x), tok: 16 (over z, y, core).
Axes of the slice: x: 2, y: 2, z: 4, core: 2. Of those that a mesh axis runs over, the one named last changes fastest.
Arguments:
- frames: bfloat16 [256, 48, 4096], P(('grp', 'tok')), parts along dimension 0, may hold values from -6 to 6
- clip_lengths: int32 [8], P('grp'), parts along dimension 0, may hold values from 1 to 56, as said below
- sequence_slot_map: int32 [2048], P(('grp', 'tok')), parts along dimension 0, may hold values from 0 to 1023, as said below
- stem_weight: bfloat16 [128, 48], replicated, may hold values from -0.875 to 0.875
- time_weight: bfloat16 [3, 128, 128], replicated, may hold values from -0.3125 to 0.3125
- norm_gain: float32 [128], replicated, may hold values from 0.1 to 1.9
- mid_weight: bfloat16 [512, 2048], replicated, may hold values from -0.125 to 0.125
- latent_weight: bfloat16 [16, 4096], replicated, may hold values from -0.09375 to 0.09375
- patch_embed_weight: bfloat16 [64, 2048], replicated, may hold values from -0.75 to 0.75
Outputs:
- dit_rows: bfloat16 [2048, 2048], P(('grp', 'tok')), parts along dimension 0
There are 2 independent parts, one for each index of `grp`. A program takes and returns all parts, laid end to end along the dimension named above; an argument that names none is the same for every part. Nothing has to cross between parts.
Inputs may be any that keep to these rules, and one draw needn't show every extreme that they name: `clip_lengths`: clips fill the 16 slabs in order: the counts ceil(length / 8) sum to 16. `sequence_slot_map`: A permutation of the 1024 sequence slots. The rows of one slab send at most 8 rows to the slots of any one slab (exactly 8 to some), and how many slab s sends to slab (s + k) mod 16 depends on k only.
All inputs are finite; a program needn't handle non-finite values.
Results may differ from a plain program's by a relative error of at most 0.0071.
Values may be sent and summed in bfloat16 or wider, within the bound.
No kernel may reach another device: no remote copies, remote signals or barrier semaphores. Data moves between devices by JAX's collectives and lax.ppermute only.
A program may use at most 128 MiB of HBM per device.

v0:
```python
import jax
import jax.numpy as jnp
from jax import lax
from jax.sharding import PartitionSpec as P

LS = 16


def shifted(block, axis, distance):
    devices = range(lax.axis_size(axis))
    route = [(i - distance, i) for i in devices if i - distance in devices]
    return lax.ppermute(block, axis, route)


def project(weight, data):
    return jnp.einsum("oc,fcp->fop", weight, data, preferred_element_type=jnp.float32)


def deliver(select, payload):
    packed = jnp.dot(select.astype(jnp.bfloat16), payload, preferred_element_type=jnp.float32)
    return packed.astype(jnp.bfloat16)


def per_device(
    frames,
    clip_lengths,
    sequence_slot_map,
    stem_weight,
    time_weight,
    norm_gain,
    mid_weight,
    latent_weight,
    patch_embed_weight,
):
    slab = lax.axis_index("tok")
    ndev = lax.axis_size("tok")
    count_frames = frames.shape[0]
    counts = (clip_lengths + 7) // 8
    ends = jnp.cumsum(counts)
    which = jnp.sum((ends <= slab).astype(jnp.int32))
    hot = jnp.arange(clip_lengths.shape[0], dtype=jnp.int32) == which
    start = jnp.sum(jnp.where(hot, ends - counts, 0))
    length = jnp.sum(jnp.where(hot, clip_lengths, 0))
    live = jnp.clip(length - count_frames * (slab - start), 0, count_frames)
    valid = (jnp.arange(count_frames, dtype=jnp.int32) < live).astype(jnp.float32)
    keep = jnp.where(slab == start, jnp.float32(0.0), jnp.float32(1.0))
    first_section = (project(stem_weight, frames) * valid[:, None, None]).astype(jnp.bfloat16)
    arrived = shifted(first_section[count_frames - 2 :], "tok", 1)
    prior = (arrived.astype(jnp.float32) * keep).astype(jnp.bfloat16)
    joined = jnp.concatenate([prior, first_section], axis=0)
    mixed = project(time_weight[0], joined[2 : count_frames + 2])
    mixed = mixed + project(time_weight[1], joined[1 : count_frames + 1])
    mixed = mixed + project(time_weight[2], joined[0:count_frames])
    meansq = jnp.mean(mixed * mixed, axis=1, keepdims=True)
    normed = mixed * lax.rsqrt(meansq + 1e-06) * norm_gain[None, :, None]
    activated = (normed * jax.nn.sigmoid(normed)).astype(jnp.bfloat16)
    channels = activated.shape[1]
    side = LS
    regrouped = activated.reshape(count_frames, channels * 16, side * side)
    deep = project(mid_weight, regrouped)
    deep = (deep * jax.nn.sigmoid(deep)).astype(jnp.bfloat16)
    latent_channels = latent_weight.shape[0]
    taps = latent_weight.reshape(latent_channels, count_frames, deep.shape[1])
    latent = jnp.einsum("ofc,fcp->op", taps, deep, preferred_element_type=jnp.float32).astype(
        jnp.bfloat16
    )
    half = side // 2
    rows = (
        latent.reshape(latent_channels, half, 2, half, 2)
        .transpose(1, 3, 0, 2, 4)
        .reshape(half * half, latent_channels * 4)
    )
    rows_count = rows.shape[0]
    capacity = max(2, 2 * rows_count // ndev)
    target = sequence_slot_map // rows_count
    place = sequence_slot_map % rows_count
    onehot = (target[:, None] == jnp.arange(ndev, dtype=jnp.int32)[None, :]).astype(jnp.int32)
    rank = jnp.sum(jnp.cumsum(onehot, axis=0) * onehot, axis=1) - 1
    send_index = target * capacity + rank
    select = send_index[None, :] == jnp.arange(ndev * capacity, dtype=jnp.int32)[:, None]
    slot_tags = jnp.sum(jnp.where(select, place[None, :] + 1, 0), axis=1).reshape(ndev, capacity)
    ordering_indices = jnp.arange(rows_count, dtype=jnp.int32)[:, None] + 1
    width = rows.shape[1]
    outgoing = deliver(select, rows).reshape(ndev, capacity, width)
    incoming, tags = (
        lax.all_to_all(outgoing, "tok", split_axis=0, concat_axis=0, tiled=True),
        lax.all_to_all(slot_tags, "tok", split_axis=0, concat_axis=0, tiled=True),
    )
    arrange = tags.reshape(1, -1) == ordering_indices
    placed = deliver(arrange, incoming.reshape(ndev * capacity, width))
    return jnp.dot(placed, patch_embed_weight, preferred_element_type=jnp.float32).astype(
        jnp.bfloat16
    )


def solution(mesh):
    placed = (
        P(("grp", "tok"), None, None),
        P("grp"),
        P(("grp", "tok")),
        P(),
        P(),
        P(),
        P(),
        P(),
        P(),
    )
    return jax.shard_map(
        per_device, mesh=mesh, in_specs=placed, out_specs=P(("grp", "tok"), None), check_vma=False
    )
```

profile of v0, /device:TPU:0, one launch (start us, length us, event | category | flops | bytes accessed | tf_op | source)
XLA Modules:
  0.0 121.0 jit_solution(15784494415079990977)
XLA Ops:
  0.0 0.8 fusion.55
  0.8 0.2 reduce-window.9
  1.0 0.6 fusion.46
  1.6 2.0 %fusion.43 = (s32[]{:T(128)}, s32[]{:T(128)}) fusion(s32[4]{0:T(128)} %param.10, s32[]{:T(128)} %fusion.46, s32[4,1]{0,1:T(1,128)S(1)} %reduce-window.9), kind=kLoop, calls=%fused_computation.61 | loop fusion | flops 86 | bytes 44 | tf_op jit(solution)/shard_map/reduce_sum | solution.py:43
  5.0 4.1 %fusion.5 = bf16[8,128,4096]{1,2,0:T(8,128)(2,1)S(1)} fusion(f32[8]{0:T(128)S(1)} %compare_convert_fusion, bf16[8,48,4096]{2,1,0:T(8,128)(2,1)S(1)} %copy-done, bf16[128,48]{0,1:T(8,128)(2,1)} %param.12), kind=kOutput, calls=%fused_computation.11 | convolution fusion | flops 411041792 | bytes 11546656 | tf_op jit(solution)/shard_map/oc,fcp->fop/dot_general | solution.py:16
  9.1 3.2 %copy-done.2 = bf16[8,128,4096]{1,2,0:T(8,128)(2,1)} copy-done((bf16[8,128,4096]{1,2,0:T(8,128)(2,1)}, bf16[8,128,4096]{1,2,0:T(8,128)(2,1)S(1)}, u32[]{:S(2)}) %copy-start.2) | copy-done | bytes 8388632
  12.4 3.8 %collective-permute-start = (bf16[2,128,4096]{1,2,0:T(8,128)(2,1)S(1)}, bf16[2,128,4096]{1,2,0:T(8,128)(2,1)}, u32[]{:S(2)}, u32[]{:S(2)}) collective-permute-start(bf16[2,128,4096]{1,2,0:T(8,128)(2,1)S(1)} %slice.24), channel_id=1, source_target_pairs={{0,1},{1,2},{2,3},{3,4},{4,5},{5,6},{6,7},{7,8},{8,9},{9,10},{10,1... | collective-permute-start | bytes 6291464 | tf_op jit(solution)/shard_map/ppermute | solution.py:12
  16.7 0.7 all_to_all.9
  17.4 5.9 %all-to-all-start = ((s32[16,1,8]{2,1,0:T(1,128)}), s32[16,1,8]{2,1,0:T(1,128)S(1)}, u32[]{:S(2)}, u32[]{:S(2)}) async-start(s32[16,1,8]{2,1,0:T(1,128)} %bitcast), calls=%async_computation | async-start | bytes 16384 | tf_op jit(solution)/shard_map/all_to_all | solution.py:87
  23.9 11.6 %fusion.29 = f32[8,4096,128]{1,2,0:T(8,128)} fusion(bf16[8,128,4096]{1,2,0:T(8,128)(2,1)} %copy-done.2, bf16[3,128,128]{2,1,0:T(8,128)(2,1)S(1)} %copy-done.4), kind=kOutput, calls=%fused_computation.33 | convolution fusion | flops 1073741824 | bytes 25198592 | tf_op jit(solution)/shard_map/oc,fcp->fop/dot_general | solution.py:16
  35.5 2.0 %multiply_convert_fusion.1 = bf16[2,128,4096]{1,2,0:T(8,128)(2,1)S(1)} fusion(bf16[2,128,4096]{1,2,0:T(8,128)(2,1)} %collective-permute-done, f32[]{:T(128)S(6)} %select_n.38), kind=kLoop, calls=%fused_computation.17 | loop fusion | flops 3145728 | bytes 4194308 | tf_op jit(solution)/shard_map/convert_element_type | solution.py:49
  37.5 7.0 %fusion.4 = f32[8,4096,128]{1,2,0:T(8,128)} fusion(bf16[8,128,4096]{1,2,0:T(8,128)(2,1)S(1)} %copy-done.3, bf16[2,128,4096]{1,2,0:T(8,128)(2,1)S(1)} %multiply_convert_fusion.1, bf16[3,128,128]{2,1,0:T(8,128)(2,1)S(1)} %copy-done.4), kind=kOutput, calls=%fused_computation.10 | convolution fusion | flops 1094713344 | bytes 27295744 | tf_op jit(solution)/shard_map/oc,fcp->fop/dot_general | solution.py:16
  44.5 20.3 %multiply_reduce_fusion = (f32[8,4096]{1,0:T(8,128)S(1)}, f32[8,4096,128]{1,2,0:T(8,128)}) fusion(bf16[3,128,128]{2,1,0:T(8,128)(2,1)S(1)} %copy-done.4, bf16[8,128,4096]{1,2,0:T(8,128)(2,1)} %copy-done.2, bf16[2,128,4096]{1,2,0:T(8,128)(2,1)S(1)} %multiply_convert_fusion.1, f32[8,4096,128]{1,2,0:T(8,128)} %fusion.29, f32[8,4096,128]{1,2,0:T(8,128)} %fusion.4), kind=kOutput, calls=%fused_computation.5 | convolution fusion | flops 1111457792 | bytes 60981248 | tf_op jit(solution)/shard_map/oc,fcp->fop/dot_general | solution.py:16
  64.8 11.6 %fusion.3 = bf16[8,128,4096]{2,1,0:T(8,128)(2,1)} fusion(f32[8,4096,128]{1,2,0:T(8,128)} %get-tuple-element.8, f32[128]{0:T(128)S(1)} %copy-done.5, f32[8,4096]{1,0:T(8,128)S(1)} %add_rsqrt_fusion), kind=kLoop, calls=%fused_computation.8 | loop fusion | flops 29360128 | bytes 25297408 | tf_op jit(solution)/shard_map/convert_element_type | solution.py:56
  76.4 13.5 %reshape.76 = bf16[8,2048,256]{2,1,0:T(8,128)(2,1)} reshape(bf16[8,128,4096]{2,1,0:T(8,128)(2,1)} %fusion.3) | data formatting | bytes 16777216 | tf_op jit(solution)/shard_map/reshape | solution.py:59
  89.9 8.9 %fusion.20 = bf16[16,256]{1,0:T(8,128)(2,1)S(1)} fusion(bf16[8,2048,256]{2,1,0:T(8,128)(2,1)} %reshape.76, bf16[512,2048]{1,0:T(8,128)(2,1)} %param.15, bf16[2,8,8,512]{3,2,1,0:T(8,128)(2,1)S(1)} %bitcast.103), kind=kOutput, calls=%fused_computation.26 | convolution fusion | flops 4333768704 | bytes 10625024 | tf_op jit(solution)/shard_map/ofc,fcp->op/dot_general | solution.py:64
  99.0 0.3 copy.43
  99.4 0.2 convolution_convert_fusion.2
  99.7 0.7 reshape.97
  100.4 11.9 %all-to-all-start.1 = ((bf16[16,2,256]{2,1,0:T(2,128)(2,1)}), bf16[16,2,256]{2,1,0:T(2,128)(2,1)S(1)}, u32[]{:S(2)}, u32[]{:S(2)}) async-start(bf16[16,2,256]{2,1,0:T(2,128)(2,1)} %reshape.97), calls=%async_computation.1 | async-start | bytes 32768 | tf_op jit(solution)/shard_map/all_to_all | solution.py:86
  112.3 0.6 broadcast.108
  112.9 0.7 reduce.4
  113.7 5.1 %all-to-all-done.1 = bf16[16,2,256]{2,1,0:T(2,128)(2,1)S(1)} async-done(((bf16[16,2,256]{2,1,0:T(2,128)(2,1)}), bf16[16,2,256]{2,1,0:T(2,128)(2,1)S(1)}, u32[]{:S(2)}, u32[]{:S(2)}) %all-to-all-start.1) | async-done | bytes 16416 | tf_op jit(solution)/shard_map/all_to_all | solution.py:86
  118.9 2.1 %convolution_convert_fusion = bf16[64,2048]{1,0:T(8,128)(2,1)} fusion(bf16[64,2048]{1,0:T(8,128)(2,1)} %param.17, bf16[16,8,64]{2,1,0:T(8,128)(2,1)S(1)} %reshape.98, s32[128]{0:T(128)S(1)} %eq.58, s32[64]{0:T(128)S(1)} %iota_add_fusion), kind=kOutput, calls=%fused_computation.19 | convolution fusion | flops 17969152 | bytes 541440 | tf_op jit(solution)/shard_map/dot_general | solution.py:91
  (32 shorter events, 1.3 us)
Async XLA Ops:
  0.0 5.0 %copy-start = (bf16[8,48,4096]{2,1,0:T(8,128)(2,1)S(1)}, bf16[8,48,4096]{2,1,0:T(8,128)(2,1)}, u32[]{:S(2)}) copy-start(bf16[8,48,4096]{2,1,0:T(8,128)(2,1)} %param.9) | copy-start | bytes 9437188
  0.0 16.2 %copy-start.7 = (s32[64]{0:T(128)S(1)}, s32[64]{0:T(128)}, u32[]{:S(2)}) copy-start(s32[64]{0:T(128)} %param.11) | copy-start | bytes 772
  0.0 23.9 %copy-start.4 = (bf16[3,128,128]{2,1,0:T(8,128)(2,1)S(1)}, bf16[3,128,128]{2,1,0:T(8,128)(2,1)}, u32[]{:S(2)}) copy-start(bf16[3,128,128]{2,1,0:T(8,128)(2,1)} %param.13) | copy-start | bytes 294916
  9.1 3.2 %copy-start.2 = (bf16[8,128,4096]{1,2,0:T(8,128)(2,1)}, bf16[8,128,4096]{1,2,0:T(8,128)(2,1)S(1)}, u32[]{:S(2)}) copy-start(bf16[8,128,4096]{1,2,0:T(8,128)(2,1)S(1)} %fusion.5) | copy-start | bytes 25165828
  12.4 23.1 %collective-permute-start = (bf16[2,128,4096]{1,2,0:T(8,128)(2,1)S(1)}, bf16[2,128,4096]{1,2,0:T(8,128)(2,1)}, u32[]{:S(2)}, u32[]{:S(2)}) collective-permute-start(bf16[2,128,4096]{1,2,0:T(8,128)(2,1)S(1)} %slice.24), channel_id=1, source_target_pairs={{0,1},{1,2},{2,3},{3,4},{4,5},{5,6},{6,7},{7,8},{8,9},{9,10},{10,1... | collective-permute-start | bytes 6291464 | tf_op jit(solution)/shard_map/ppermute | solution.py:12
  17.4 83.0 %all-to-all-start = ((s32[16,1,8]{2,1,0:T(1,128)}), s32[16,1,8]{2,1,0:T(1,128)S(1)}, u32[]{:S(2)}, u32[]{:S(2)}) async-start(s32[16,1,8]{2,1,0:T(1,128)} %bitcast), calls=%async_computation | async-start | bytes 16384 | tf_op jit(solution)/shard_map/all_to_all | solution.py:87
  23.9 13.6 %copy-start.3 = (bf16[8,128,4096]{1,2,0:T(8,128)(2,1)S(1)}, bf16[8,128,4096]{1,2,0:T(8,128)(2,1)}, u32[]{:S(2)}) copy-start(bf16[8,128,4096]{1,2,0:T(8,128)(2,1)} %copy-done.2) | copy-start | bytes 25165828
  44.5 20.3 %copy-start.5 = (f32[128]{0:T(128)S(1)}, f32[128]{0:T(128)}, u32[]{:S(2)}) copy-start(f32[128]{0:T(128)} %param.14) | copy-start | bytes 1540
  76.4 13.5 %copy-start.6 = (bf16[16,4096]{1,0:T(8,128)(2,1)S(1)}, bf16[16,4096]{1,0:T(8,128)(2,1)}, u32[]{:S(2)}) copy-start(bf16[16,4096]{1,0:T(8,128)(2,1)} %param.16) | copy-start | bytes 393220
  89.9 31.1 %copy-start.1 = (bf16[8,48,4096]{2,1,0:T(8,128)(2,1)S(1)}, bf16[8,48,4096]{2,1,0:T(8,128)(2,1)}, u32[]{:S(2)}) copy-start(bf16[8,48,4096]{2,1,0:T(8,128)(2,1)} %param.9) | copy-start | bytes 9437188
  100.4 18.4 %all-to-all-start.1 = ((bf16[16,2,256]{2,1,0:T(2,128)(2,1)}), bf16[16,2,256]{2,1,0:T(2,128)(2,1)S(1)}, u32[]{:S(2)}, u32[]{:S(2)}) async-start(bf16[16,2,256]{2,1,0:T(2,128)(2,1)} %reshape.97), calls=%async_computation.1 | async-start | bytes 32768 | tf_op jit(solution)/shard_map/all_to_all | solution.py:86
where the time goes:
time: 122 us; the launch traced here: 121 us
  matrix products  54.1 us (44%)
  starting transfers between devices  21.5 us (18%)
  local copies, waits for them, and re-layouts  19.7 us (16%)
  other arithmetic  18.4 us (15%)
  waiting for transfers between devices  5.1 us (4%)
  between operations  2.09 us (2%)
    dot_general x4, matrix products, project(): jnp.einsum('oc,fcp->fop', weight, data, preferred_element_type=jnp.float32)  43 us
    reshape x1, local copies, waits for them, and re-layouts, per_device(): regrouped = activated.reshape(count_frames, channels * 16, side * side)  13.5 us
    all_to_all x1, starting transfers between devices, per_device(): lax.all_to_all(outgoing, 'tok', split_axis=0, concat_axis=0, tiled=True)  11.9 us
    convert_element_type x1, other arithmetic, per_device(): activated = (normed * jax.nn.sigmoid(normed)).astype(jnp.bfloat16)  11.6 us
    dot_general x1, matrix products, per_device(): jnp.einsum('ofc,fcp->op', taps, deep, preferred_element_type=jnp.float32)  8.91 us
    all_to_all x1, starting transfers between devices, per_device(): lax.all_to_all(slot_tags, 'tok', split_axis=0, concat_axis=0, tiled=True)  5.88 us
    all_to_all x1, waiting for transfers between devices, per_device(): lax.all_to_all(outgoing, 'tok', split_axis=0, concat_axis=0, tiled=True)  5.09 us
    unnamed x18, local copies, waits for them, and re-layouts  4.03 us
  transfers between devices with their start and end apart: 3, of which 1 were waited for; matrix products, arithmetic and copies ran while one was open for 65% of the time, Pallas kernels for 0%

commit v1 on v0

v1 whole, which is shorter than its diff:
```python
import functools

import jax
import jax.numpy as jnp
from jax import lax
from jax.experimental import pallas as pl
from jax.experimental.pallas import tpu as pltpu
from jax.sharding import PartitionSpec as P

LS = 16
F32 = jnp.float32
BF16 = jnp.bfloat16


def iota(shape, dimension):
    return lax.broadcasted_iota(jnp.int32, shape, dimension)


def dot(a, b):
    return jnp.dot(a, b, preferred_element_type=F32)


def band_weights(stem, time, wband, tiles):
    channels, cin = stem.shape
    taps = time.shape[0]
    window = taps + 1
    rows = iota((cin, window * cin), 0)
    columns = iota((cin, window * cin), 1)
    spread = [
        dot(stem, (columns == rows + j * cin).astype(BF16)).astype(BF16) for j in range(window)
    ]
    for half in range(2):
        total = None
        for k in range(taps):
            part = dot(time[k], spread[taps - 1 - k + half])
            total = part if total is None else total + part
        wband[half * channels : (half + 1) * channels, :] = total


def clip_state(clip_ref, slab, count_frames, clips):
    live = jnp.int32(0)
    first = jnp.int32(0)
    end = jnp.int32(0)
    for c in range(clips):
        length = clip_ref[c]
        begin = end
        end = begin + (length + (count_frames - 1)) // count_frames
        mine = jnp.logical_and(slab >= begin, slab < end)
        left = jnp.clip(length - count_frames * (slab - begin), 0, count_frames)
        live = jnp.where(mine, left, live)
        first = jnp.where(mine, (slab == begin).astype(jnp.int32), first)
    return live, first


def routed(latent, slots_ref, ndev, capacity, side):
    channels, cells = latent.shape
    rows = slots_ref.shape[1]
    half = side // 2
    slots = slots_ref[...].astype(F32)
    target_row = jnp.floor(slots / rows)
    i0, i1 = iota((rows, rows), 0), iota((rows, rows), 1)
    slot_col = jnp.sum(jnp.where(i0 == i1, jnp.broadcast_to(slots, (rows, rows)), 0.0), axis=1, keepdims=True)
    target_col = jnp.floor(slot_col / rows)
    place_col = slot_col - target_col * rows
    same = jnp.logical_and(target_col == target_row, i1 < i0)
    rank = jnp.sum(jnp.where(same, 1.0, 0.0), axis=1, keepdims=True)
    send_col = target_col * capacity + rank
    cell = iota((rows, cells), 1)
    row_of_cell = (cell // (2 * side)) * half + (cell % side) // 2
    mine = row_of_cell == iota((rows, cells), 0)
    send = jnp.sum(jnp.where(mine, send_col, 0.0), axis=0, keepdims=True)
    place = jnp.sum(jnp.where(mine, place_col, 0.0), axis=0, keepdims=True)
    lanes = 128
    pick = (iota((ndev * capacity, cells), 0).astype(F32) == send).astype(BF16)
    feature, cell = iota((lanes, cells), 0), iota((lanes, cells), 1)
    sub = (cell // side) % 2 * 2 + cell % 2
    spread = (iota((lanes, channels), 0) // 4 == iota((lanes, channels), 1)).astype(BF16)
    values = dot(spread, latent)
    values = jnp.where(feature % 4 == sub, values, 0.0)
    tags = jnp.where(jnp.logical_and(feature == 4 * channels, sub == 0), place + 1.0, 0.0)
    values = (values + tags).astype(BF16)
    return lax.dot_general(pick, values, (((1,), (1,)), ((), ())), preferred_element_type=F32).astype(BF16)


def encode_kernel(
    ndev,
    capacity,
    side,
    clips,
    slab_ref,
    clip_ref,
    prior_ref,
    frames_ref,
    slots_ref,
    stem_ref,
    time_ref,
    gain_ref,
    mid_ref,
    latent_ref,
    out_ref,
    joined,
    wband,
    wmask,
    midp,
    regrouped,
    total,
):
    count_frames, cin, positions = frames_ref.shape
    taps = time_ref.shape[0]
    channels = stem_ref.shape[0]
    deep = mid_ref.shape[0]
    cells = side * side
    patches = positions // cells
    pairs = count_frames // 2
    block = 16
    live, first = clip_state(clip_ref, slab_ref[0], count_frames, clips)
    band_weights(stem_ref[...], time_ref[...], wband, None)
    frame_of = iota((2 * channels, 4 * cin), 1)
    offset = (
        (frame_of >= cin).astype(jnp.int32)
        + (frame_of >= 2 * cin).astype(jnp.int32)
        + (frame_of >= 3 * cin).astype(jnp.int32)
        - 2
    )
    for p in range(pairs):
        at = offset + 2 * p
        kept = jnp.where(at < 0, 1 - first, (at < live).astype(jnp.int32))
        wmask[p] = jnp.where(kept > 0, wband[...], 0.0).astype(BF16)
    joined[0 : 2 * cin, :] = prior_ref[...].reshape(2 * cin, positions)
    for f in range(count_frames):
        joined[(2 + f) * cin : (3 + f) * cin, :] = frames_ref[f]
    width = block * patches
    i0, i1 = iota((width, width), 0), iota((width, width), 1)
    permute = (i0 == (i1 % block) * patches + i1 // block).astype(BF16)
    for b in range(channels // block):
        midp[:, b * width : (b + 1) * width] = dot(mid_ref[:, b * width : (b + 1) * width], permute).astype(BF16)
    gain = gain_ref[...] * 0.5
    total[...] = jnp.zeros_like(total)

    def pair(p, carry):
        start = pl.multiple_of(p * 2 * cin, 2 * cin)
        for ab in range(patches):
            mixed = dot(wmask[p], joined[pl.ds(start, 4 * cin), ab * cells : (ab + 1) * cells])
            for half in range(2):
                h = mixed[half * channels : (half + 1) * channels]
                meansq = jnp.sum(h * h, axis=0, keepdims=True) * (1.0 / channels)
                v = h * lax.rsqrt(meansq + 1e-06) * gain
                u = (v * jnp.tanh(v) + v).astype(BF16)
                for b in range(channels // block):
                    row = (b * patches + ab) * block
                    regrouped[row : row + block, half * cells : (half + 1) * cells] = u[
                        b * block : (b + 1) * block
                    ]
        g = dot(midp[...], regrouped[...]) * 0.5
        m = (g * jnp.tanh(g) + g).astype(BF16)
        for half in range(2):
            at = pl.multiple_of((2 * p + half) * deep, deep)
            total[...] += dot(latent_ref[:, pl.ds(at, deep)], m[:, half * cells : (half + 1) * cells])
        return carry

    lax.fori_loop(0, pairs, pair, 0)
    out_ref[...] = routed(total[...].astype(BF16), slots_ref, ndev, capacity, side)


def embed_kernel(incoming_ref, weight_ref, out_ref):
    rows = out_ref.shape[0]
    features = weight_ref.shape[0]
    incoming = incoming_ref[...]
    tags = incoming[:, features : features + 1].astype(F32)
    arrange = (tags == (iota((incoming.shape[0], rows), 1) + 1).astype(F32)).astype(BF16)
    placed = lax.dot_general(arrange, incoming, (((0,), (0,)), ((), ())), preferred_element_type=F32)
    out_ref[...] = dot(placed[:, :features].astype(BF16), weight_ref[...]).astype(BF16)


def per_device(
    frames,
    clip_lengths,
    sequence_slot_map,
    stem_weight,
    time_weight,
    norm_gain,
    mid_weight,
    latent_weight,
    patch_embed_weight,
):
    slab = lax.axis_index("tok")
    ndev = lax.axis_size("tok")
    count_frames, cin, positions = frames.shape
    rows_count = sequence_slot_map.shape[0]
    capacity = max(2, 2 * rows_count // ndev)
    side = LS
    channels = stem_weight.shape[0]
    latents = latent_weight.shape[0]
    deep = mid_weight.shape[0]
    prior = lax.ppermute(frames[count_frames - 2 :], "tok", [(i, i + 1) for i in range(ndev - 1)])
    vmem = pl.BlockSpec(memory_space=pltpu.VMEM)
    smem = pl.BlockSpec(memory_space=pltpu.SMEM)
    outgoing = pl.pallas_call(
        functools.partial(encode_kernel, ndev, capacity, side, clip_lengths.shape[0]),
        out_shape=jax.ShapeDtypeStruct((ndev * capacity, 128), BF16),
        in_specs=[smem, smem] + [vmem] * 8,
        out_specs=vmem,
        scratch_shapes=[
            pltpu.VMEM(((count_frames + 2) * cin, positions), BF16),
            pltpu.VMEM((2 * channels, 4 * cin), F32),
            pltpu.VMEM((count_frames // 2, 2 * channels, 4 * cin), BF16),
            pltpu.VMEM(mid_weight.shape, BF16),
            pltpu.VMEM((mid_weight.shape[1], 2 * side * side), BF16),
            pltpu.VMEM((latents, side * side), F32),
        ],
        compiler_params=pltpu.CompilerParams(vmem_limit_bytes=56 << 20),
        name="encode",
    )(
        slab.astype(jnp.int32).reshape(1),
        clip_lengths,
        prior,
        frames,
        sequence_slot_map.reshape(1, rows_count),
        stem_weight,
        time_weight,
        norm_gain.reshape(channels, 1),
        mid_weight,
        latent_weight,
    )
    incoming = lax.all_to_all(
        outgoing.reshape(ndev, capacity, 128), "tok", split_axis=0, concat_axis=0, tiled=True
    )
    return pl.pallas_call(
        embed_kernel,
        out_shape=jax.ShapeDtypeStruct((rows_count, patch_embed_weight.shape[1]), BF16),
        in_specs=[vmem, vmem],
        out_specs=vmem,
        name="embed",
    )(incoming.reshape(ndev * capacity, 128), patch_embed_weight)


def solution(mesh):
    placed = (
        P(("grp", "tok"), None, None),
        P("grp"),
        P(("grp", "tok")),
        P(),
        P(),
        P(),
        P(),
        P(),
        P(),
    )
    return jax.shard_map(
        per_device, mesh=mesh, in_specs=placed, out_specs=P(("grp", "tok"), None), check_vma=False
    )
```

time: 122 us -> 45.6 us (0.37)
  matrix products: 54.1 us -> 0 us
  blocking collectives: 0 us -> 22.2 us
  starting transfers between devices: 21.5 us -> 2.45 us
  other arithmetic: 18.4 us -> 0 us
  Pallas kernels: 0 us -> 15.8 us
  local copies, waits for them, and re-layouts: 19.7 us -> 4.86 us
  waiting for transfers between devices: 5.1 us -> 0.01 us
  between operations: 2.09 us -> 0.02 us
    dot_general x7 -> x0, matrix products: 54.1 us -> none  [the longest x4 43 us: project(): jnp.einsum('oc,fcp->fop', weight, data, preferred_element_type=jnp.float32)]
    all_to_all x0 -> x1, blocking collectives: none -> 22.2 us  [per_device(): lax.all_to_all(outgoing.reshape(ndev, capacity, 128), 'tok', split_axis=0...]
    all_to_all x2 -> x0, starting transfers between devices: 17.8 us -> none  [the longest x1 11.9 us: per_device(): lax.all_to_all(outgoing, 'tok', split_axis=0, concat_axis=0, tiled=True)]
    pallas_call x0 -> x2, Pallas kernels: none -> 15.8 us  [the longest x1 13.7 us: per_device(): pl.pallas_call(functools.partial(encode_kernel, ndev, capacity, side, cli...]
    convert_element_type x4 -> x0, other arithmetic: 13.6 us -> none  [the longest x1 11.6 us: per_device(): activated = (normed * jax.nn.sigmoid(normed)).astype(jnp.bfloat16)]
    reshape x2 -> x1, local copies, waits for them, and re-layouts: 13.6 us -> 1.39 us  [per_device(): norm_gain.reshape(channels, 1)]
    all_to_all x2 -> x0, waiting for transfers between devices: 5.09 us -> none  [the longest x1 5.09 us: per_device(): lax.all_to_all(outgoing, 'tok', split_axis=0, concat_axis=0, tiled=True)]
    reduce_sum x4 -> x0, other arithmetic: 2.94 us -> none  [the longest x1 2.02 us: per_device(): length = jnp.sum(jnp.where(hot, clip_lengths, 0))]
  transfers between devices with their start and end apart: 3 -> 1, of which waited for: 1 -> 0; matrix products, arithmetic and copies ran while one was open for 65% -> 6% of each run, Pallas kernels for 0% -> 0%
where the time goes in v1:
time: 45.6 us; the launch traced here: 45.3 us
  blocking collectives  22.2 us (49%)
  Pallas kernels  15.8 us (35%)
  local copies, waits for them, and re-layouts  4.86 us (11%)
  starting transfers between devices  2.45 us (5%)
    all_to_all x1, blocking collectives, per_device(): lax.all_to_all(outgoing.reshape(ndev, capacity, 128), 'tok', split_axis=0...  22.2 us
    pallas_call x1, Pallas kernels, per_device(): pl.pallas_call(functools.partial(encode_kernel, ndev, capacity, side, cli...  13.7 us
    ppermute x1, starting transfers between devices, per_device(): lax.ppermute(frames[count_frames - 2:], 'tok', [(i, i + 1) for i in range...  2.45 us
    unnamed x3, local copies, waits for them, and re-layouts  2.29 us
    pallas_call x1, Pallas kernels, per_device(): pl.pallas_call(embed_kernel, out_shape=jax.ShapeDtypeStruct((rows_count,...  2.13 us
    reshape x1, local copies, waits for them, and re-layouts, per_device(): norm_gain.reshape(channels, 1)  1.39 us
    slice x1, local copies, waits for them, and re-layouts, per_device(): frames[count_frames - 2:]  1.18 us
  transfers between devices with their start and end apart: 1, of which 0 were waited for; matrix products, arithmetic and copies ran while one was open for 6% of the time, Pallas kernels for 0%

profile of v1, /device:TPU:0, one launch (start us, length us, event | category | flops | bytes accessed | tf_op | source)
XLA Modules:
  0.0 45.3 jit_solution(6146967405450996688)
XLA Ops:
  0.0 1.2 %slice.3 = bf16[2,48,4096]{2,1,0:T(8,128)(2,1)S(1)} slice(bf16[8,48,4096]{2,1,0:T(8,128)(2,1)} %frames_ref.1), slice={[6:8], [0:48], [0:4096]} | slice | bytes 1572864 | tf_op jit(solution)/shard_map/slice | solution.py:195
  1.2 2.4 %collective-permute-start = (bf16[2,48,4096]{2,1,0:T(8,128)(2,1)S(1)}, bf16[2,48,4096]{2,1,0:T(8,128)(2,1)S(1)}, u32[]{:S(2)}, u32[]{:S(2)}) collective-permute-start(bf16[2,48,4096]{2,1,0:T(8,128)(2,1)S(1)} %slice.3), channel_id=1, source_target_pairs={{0,1},{1,2},{2,3},{3,4},{4,5},{5,6},{6,7},{7,8},{8,9},{9,10},{10,1... | collective-permute-start | bytes 2359304 | tf_op jit(solution)/shard_map/ppermute | solution.py:195
  3.6 1.4 %copy.11.gain_ref = f32[128,1]{1,0:T(8,128)} copy(f32[128,1]{0,1:T(1,128)} %bitcast.7) | data formatting | bytes 1024 | tf_op jit(solution)/shard_map/reshape | solution.py:221
  5.0 1.4 %copy.10.stem_ref = bf16[128,48]{1,0:T(8,128)(2,1)} copy(bf16[128,48]{0,1:T(8,128)(2,1)} %param.12) | data formatting | bytes 24576 | tf_op args[3]
  6.4 0.0 collective-permute-done.prior_ref
  6.4 0.0 copy-start
  6.5 0.9 %copy-done = bf16[2,48,4096]{2,1,0:T(8,128)(2,1)} copy-done((bf16[2,48,4096]{2,1,0:T(8,128)(2,1)}, bf16[2,48,4096]{2,1,0:T(8,128)(2,1)S(1)}, u32[]{:S(2)}) %copy-start) | copy-done | bytes 786456
  7.3 13.7 %encode.1 = bf16[128,128]{1,0:T(8,128)(2,1)} custom-call(s32[1]{0:T(128)} %bitcast.slab_ref, s32[4]{0:T(128)} %clip_ref.1, bf16[2,48,4096]{2,1,0:T(8,128)(2,1)} %copy-done, bf16[8,48,4096]{2,1,0:T(8,128)(2,1)} %frames_ref.1, s32[1,64]{1,0:T(1,128)} %bitcast.8, bf16[128,48]{1,0:T(8,128)(2,1)} %copy.10.stem_ref, bf16[3,128,128]{2,1,0:T(8,128)(2,1)} %time_ref.1, ...), custom_call_target="tpu_custom_call" | custom-call | tf_op jit(solution)/shard_map/encode/pallas_call | solution.py:198
  21.0 22.2 %all_to_all.5 = bf16[16,8,128]{2,1,0:T(8,128)(2,1)} all-to-all(bf16[16,8,128]{2,1,0:T(8,128)(2,1)} %bitcast.5), channel_id=1, replica_groups=mesh['grp'=2,'tok'=16] {'tok'}, dimensions={0} | all-to-all | bytes 65536 | tf_op jit(solution)/shard_map/all_to_all | solution.py:225
  43.2 2.1 %embed.1 = bf16[64,2048]{1,0:T(8,128)(2,1)} custom-call(bf16[128,128]{1,0:T(8,128)(2,1)} %bitcast.6, bf16[64,2048]{1,0:T(8,128)(2,1)} %weight_ref.1), custom_call_target="tpu_custom_call" | custom-call | tf_op jit(solution)/shard_map/embed/pallas_call | solution.py:228
Async XLA Ops:
  1.2 5.3 %collective-permute-start = (bf16[2,48,4096]{2,1,0:T(8,128)(2,1)S(1)}, bf16[2,48,4096]{2,1,0:T(8,128)(2,1)S(1)}, u32[]{:S(2)}, u32[]{:S(2)}) collective-permute-start(bf16[2,48,4096]{2,1,0:T(8,128)(2,1)S(1)} %slice.3), channel_id=1, source_target_pairs={{0,1},{1,2},{2,3},{3,4},{4,5},{5,6},{6,7},{7,8},{8,9},{9,10},{10,1... | collective-permute-start | bytes 2359304 | tf_op jit(solution)/shard_map/ppermute | solution.py:195
  6.4 0.9 %copy-start = (bf16[2,48,4096]{2,1,0:T(8,128)(2,1)}, bf16[2,48,4096]{2,1,0:T(8,128)(2,1)S(1)}, u32[]{:S(2)}) copy-start(bf16[2,48,4096]{2,1,0:T(8,128)(2,1)S(1)} %collective-permute-done.prior_ref) | copy-start | bytes 2359300

commit v2 on v1

v2 whole, which is shorter than its diff:
```python
import functools

import jax
import jax.numpy as jnp
from jax import lax
from jax.experimental import pallas as pl
from jax.experimental.pallas import tpu as pltpu
from jax.sharding import PartitionSpec as P

LS = 16
VMEM_BYTES = 24 << 20
F32 = jnp.float32
BF16 = jnp.bfloat16


def iota(shape, dimension):
    return lax.broadcasted_iota(jnp.int32, shape, dimension)


def dot(a, b):
    return jnp.dot(a, b, preferred_element_type=F32)


def band_weights(stem_ref, time_ref):
    cin, channels = stem_ref.shape
    taps = time_ref.shape[0]
    window = taps + 1
    rows = iota((cin, window * cin), 0)
    columns = iota((cin, window * cin), 1)
    spread = []
    for j in range(window):
        place = (columns == rows + j * cin).astype(BF16)
        spread.append(
            lax.dot_general(
                stem_ref[...], place, (((0,), (0,)), ((), ())), preferred_element_type=F32
            ).astype(BF16)
        )
    halves = []
    for half in range(2):
        total = None
        for k in range(taps):
            part = dot(time_ref[k], spread[taps - 1 - k + half])
            total = part if total is None else total + part
        halves.append(total)
    return jnp.concatenate(halves, axis=0)


def masked(band, first, live, pair, cin):
    column = iota(band.shape, 1)
    at = (
        (column >= cin).astype(jnp.int32)
        + (column >= 2 * cin).astype(jnp.int32)
        + (column >= 3 * cin).astype(jnp.int32)
        + (2 * pair - 2)
    )
    kept = jnp.where(at < 0, 1 - first, (at < live).astype(jnp.int32))
    return jnp.where(kept > 0, band, 0.0).astype(BF16)


def permuted(mid_ref, midp, patches, block):
    width = block * patches
    i0, i1 = iota((width, width), 0), iota((width, width), 1)
    permute = (i0 == (i1 % block) * patches + i1 // block).astype(BF16)
    for b in range(mid_ref.shape[1] // width):
        at = slice(b * width, (b + 1) * width)
        midp[:, at] = dot(mid_ref[:, at], permute).astype(BF16)


def column_of(row):
    n = row.shape[1]
    return jnp.sum(
        jnp.where(iota((n, n), 0) == iota((n, n), 1), jnp.broadcast_to(row, (n, n)), 0.0),
        axis=1,
        keepdims=True,
    )


def activate(mixed, gain, regrouped, ab, patches, block):
    channels = gain.shape[0]
    cells = mixed.shape[1]
    for half in range(2):
        h = mixed[half * channels : (half + 1) * channels]
        meansq = jnp.sum(h * h, axis=0, keepdims=True) * (1.0 / channels)
        v = h * lax.rsqrt(meansq + 1e-06) * gain
        u = (v * jnp.tanh(v) + v).astype(BF16)
        for b in range(channels // block):
            row = (b * patches + ab) * block
            regrouped[row : row + block, half * cells : (half + 1) * cells] = u[
                b * block : (b + 1) * block
            ]


def deepen(midp, regrouped, taps):
    g = dot(midp[...], regrouped[...]) * 0.5
    m = (g * jnp.tanh(g) + g).astype(BF16)
    deep, cells = m.shape[0], m.shape[1] // 2
    return dot(taps[0], m[:, :cells]) + dot(taps[1], m[:, cells:])


def clip_state(clip_ref, slab, count_frames, clips):
    live = jnp.int32(0)
    first = jnp.int32(0)
    end = jnp.int32(0)
    for c in range(clips):
        length = clip_ref[c]
        begin = end
        end = begin + (length + (count_frames - 1)) // count_frames
        mine = jnp.logical_and(slab >= begin, slab < end)
        left = jnp.clip(length - count_frames * (slab - begin), 0, count_frames)
        live = jnp.where(mine, left, live)
        first = jnp.where(mine, (slab == begin).astype(jnp.int32), first)
    return live, first


def routed(latent, slots_ref, ndev, capacity, side):
    channels, cells = latent.shape
    rows = slots_ref.shape[1]
    half = side // 2
    slots = slots_ref[...].astype(F32)
    target_row = jnp.floor(slots / rows)
    i0, i1 = iota((rows, rows), 0), iota((rows, rows), 1)
    slot_col = jnp.sum(jnp.where(i0 == i1, jnp.broadcast_to(slots, (rows, rows)), 0.0), axis=1, keepdims=True)
    target_col = jnp.floor(slot_col / rows)
    place_col = slot_col - target_col * rows
    same = jnp.logical_and(target_col == target_row, i1 < i0)
    rank = jnp.sum(jnp.where(same, 1.0, 0.0), axis=1, keepdims=True)
    send_col = target_col * capacity + rank
    cell = iota((rows, cells), 1)
    row_of_cell = (cell // (2 * side)) * half + (cell % side) // 2
    mine = row_of_cell == iota((rows, cells), 0)
    send = jnp.sum(jnp.where(mine, send_col, 0.0), axis=0, keepdims=True)
    place = jnp.sum(jnp.where(mine, place_col, 0.0), axis=0, keepdims=True)
    lanes = 128
    pick = (iota((ndev * capacity, cells), 0).astype(F32) == send).astype(BF16)
    feature, cell = iota((lanes, cells), 0), iota((lanes, cells), 1)
    sub = (cell // side) % 2 * 2 + cell % 2
    spread = (iota((lanes, channels), 0) // 4 == iota((lanes, channels), 1)).astype(BF16)
    values = dot(spread, latent)
    values = jnp.where(feature % 4 == sub, values, 0.0)
    tags = jnp.where(jnp.logical_and(feature == 4 * channels, sub == 0), place + 1.0, 0.0)
    values = (values + tags).astype(BF16)
    return lax.dot_general(pick, values, (((1,), (1,)), ((), ())), preferred_element_type=F32).astype(BF16)


def rest_kernel(
    clips, slab_ref, clip_ref, frames_ref, stem_ref, time_ref, gain_ref, mid_ref, latent_ref,
    total_ref, midp, wfirst_ref, wmask, regrouped,
):
    cin = stem_ref.shape[0]
    count_frames = frames_ref.shape[0] // cin
    deep = mid_ref.shape[0]
    channels = stem_ref.shape[1]
    patches = mid_ref.shape[1] // channels
    cells = frames_ref.shape[1] // patches
    pairs = count_frames // 2
    block = 16
    live, first = clip_state(clip_ref, slab_ref[0], count_frames, clips)
    band = band_weights(stem_ref, time_ref)
    wfirst_ref[...] = masked(band, first, live, 0, cin)
    for p in range(1, pairs):
        wmask[p - 1] = masked(band, first, live, p, cin)
    permuted(mid_ref, midp, patches, block)
    gain = column_of(gain_ref[...]) * 0.5
    total_ref[...] = jnp.zeros_like(total_ref)

    def pair(p, carry):
        start = pl.multiple_of((p - 1) * 2 * cin, 2 * cin)
        for ab in range(patches):
            mixed = dot(wmask[p - 1], frames_ref[pl.ds(start, 4 * cin), ab * cells : (ab + 1) * cells])
            activate(mixed, gain, regrouped, ab, patches, block)
        taps = [
            latent_ref[:, pl.ds(pl.multiple_of((2 * p + half) * deep, deep), deep)]
            for half in range(2)
        ]
        total_ref[...] += deepen(midp, regrouped, taps)
        return carry

    lax.fori_loop(1, pairs, pair, 0)


def first_kernel(
    ndev, capacity, side, prior_ref, frames_ref, slots_ref, gain_ref, latent_ref, total_ref, midp,
    wfirst_ref, out_ref, regrouped,
):
    channels = gain_ref.shape[1]
    deep = midp.shape[0]
    patches = midp.shape[1] // channels
    cells = prior_ref.shape[1] // patches
    half_rows = prior_ref.shape[0]
    gain = column_of(gain_ref[...]) * 0.5
    for ab in range(patches):
        at = slice(ab * cells, (ab + 1) * cells)
        mixed = dot(wfirst_ref[:, :half_rows], prior_ref[:, at]) + dot(
            wfirst_ref[:, half_rows:], frames_ref[0:half_rows, at]
        )
        activate(mixed, gain, regrouped, ab, patches, 16)
    latent = total_ref[...] + deepen(
        midp, regrouped, [latent_ref[:, :deep], latent_ref[:, deep : 2 * deep]]
    )
    out_ref[...] = routed(latent.astype(BF16), slots_ref, ndev, capacity, side)


def embed_kernel(incoming_ref, weight_ref, out_ref):
    rows = out_ref.shape[0]
    features = weight_ref.shape[0]
    incoming = incoming_ref[...]
    tags = incoming[:, features : features + 1].astype(F32)
    arrange = (tags == (iota((incoming.shape[0], rows), 1) + 1).astype(F32)).astype(BF16)
    placed = lax.dot_general(arrange, incoming, (((0,), (0,)), ((), ())), preferred_element_type=F32)
    out_ref[...] = dot(placed[:, :features].astype(BF16), weight_ref[...]).astype(BF16)


def per_device(
    frames,
    clip_lengths,
    sequence_slot_map,
    stem_weight,
    time_weight,
    norm_gain,
    mid_weight,
    latent_weight,
    patch_embed_weight,
):
    slab = lax.axis_index("tok")
    ndev = lax.axis_size("tok")
    count_frames, cin, positions = frames.shape
    rows_count = sequence_slot_map.shape[0]
    capacity = max(2, 2 * rows_count // ndev)
    side = LS
    channels = stem_weight.shape[0]
    latents = latent_weight.shape[0]
    deep = mid_weight.shape[0]
    prior = lax.ppermute(frames[count_frames - 2 :], "tok", [(i, i + 1) for i in range(ndev - 1)])
    vmem = pl.BlockSpec(memory_space=pltpu.VMEM)
    smem = pl.BlockSpec(memory_space=pltpu.SMEM)
    stacked = frames.reshape(count_frames * cin, positions)
    gain = norm_gain.reshape(1, channels)
    cells = side * side
    flops = 2 * positions * 2 * channels * 4 * cin + 4 * deep * cells * mid_weight.shape[1]
    regrouped = pltpu.VMEM((mid_weight.shape[1], 2 * cells), BF16)
    total, midp, wfirst = pl.pallas_call(
        functools.partial(rest_kernel, clip_lengths.shape[0]),
        out_shape=[
            jax.ShapeDtypeStruct((latents, cells), F32),
            jax.ShapeDtypeStruct(mid_weight.shape, BF16),
            jax.ShapeDtypeStruct((2 * channels, 4 * cin), BF16),
        ],
        in_specs=[smem, smem] + [vmem] * 6,
        out_specs=[vmem] * 3,
        scratch_shapes=[
            pltpu.VMEM((count_frames // 2 - 1, 2 * channels, 4 * cin), BF16),
            regrouped,
        ],
        compiler_params=pltpu.CompilerParams(vmem_limit_bytes=VMEM_BYTES),
        cost_estimate=pl.CostEstimate(
            flops=3 * flops, bytes_accessed=10 << 20, transcendentals=3 * positions * 256
        ),
        name="rest",
    )(
        slab.astype(jnp.int32).reshape(1),
        clip_lengths,
        stacked,
        stem_weight.T,
        time_weight,
        gain,
        mid_weight,
        latent_weight,
    )
    outgoing = pl.pallas_call(
        functools.partial(first_kernel, ndev, capacity, side),
        out_shape=jax.ShapeDtypeStruct((ndev * capacity, 128), BF16),
        in_specs=[vmem] * 8,
        out_specs=vmem,
        scratch_shapes=[regrouped],
        compiler_params=pltpu.CompilerParams(vmem_limit_bytes=VMEM_BYTES),
        name="first",
    )(
        prior.reshape(2 * cin, positions),
        stacked,
        sequence_slot_map.reshape(1, rows_count),
        gain,
        latent_weight,
        total,
        midp,
        wfirst,
    )
    incoming = lax.all_to_all(
        outgoing.reshape(ndev, capacity, 128), "tok", split_axis=0, concat_axis=0, tiled=True
    )
    return pl.pallas_call(
        embed_kernel,
        out_shape=jax.ShapeDtypeStruct((rows_count, patch_embed_weight.shape[1]), BF16),
        in_specs=[vmem, vmem],
        out_specs=vmem,
        name="embed",
    )(incoming.reshape(ndev * capacity, 128), patch_embed_weight)


def solution(mesh):
    placed = (
        P(("grp", "tok"), None, None),
        P("grp"),
        P(("grp", "tok")),
        P(),
        P(),
        P(),
        P(),
        P(),
        P(),
    )
    return jax.shard_map(
        per_device, mesh=mesh, in_specs=placed, out_specs=P(("grp", "tok"), None), check_vma=False
    )
```

time: 45.6 us -> 39.3 us (0.86)
  blocking collectives: 22.2 us -> 13.7 us
  local copies, waits for them, and re-layouts: 4.86 us -> 8.49 us
  Pallas kernels: 15.8 us -> 14.2 us
    all_to_all x1, blocking collectives: 22.2 us -> 13.7 us  [per_device(): lax.all_to_all(outgoing.reshape(ndev, capacity, 128), 'tok', split_axis=0...]
    unnamed x3 -> x20, local copies, waits for them, and re-layouts: 2.29 us -> 7.31 us
    pallas_call x1 -> x2, Pallas kernels: 13.7 us -> 12.1 us  [the longest x1 8.84 us: per_device(): pl.pallas_call(functools.partial(rest_kernel, clip_lengths.shape[0]), out...]
    reshape x1 -> x0, local copies, waits for them, and re-layouts: 1.39 us -> none  [per_device(): norm_gain.reshape(channels, 1)]
  transfers between devices with their start and end apart: 1 -> 1, of which waited for: 0 -> 0; matrix products, arithmetic and copies ran while one was open for 6% -> 0% of each run, Pallas kernels for 0% -> 23%
where the time goes in v2:
time: 39.3 us; the launch traced here: 38.9 us
  Pallas kernels  14.2 us (36%)
  blocking collectives  13.7 us (35%)
  local copies, waits for them, and re-layouts  8.49 us (22%)
  starting transfers between devices  2.45 us (6%)
    all_to_all x1, blocking collectives, per_device(): lax.all_to_all(outgoing.reshape(ndev, capacity, 128), 'tok', split_axis=0...  13.7 us
    pallas_call x1, Pallas kernels, per_device(): pl.pallas_call(functools.partial(rest_kernel, clip_lengths.shape[0]), out...  8.84 us
    unnamed x20, local copies, waits for them, and re-layouts  7.31 us
    pallas_call x1, Pallas kernels, per_device(): pl.pallas_call(functools.partial(first_kernel, ndev, capacity, side), out...  3.24 us
    ppermute x1, starting transfers between devices, per_device(): lax.ppermute(frames[count_frames - 2:], 'tok', [(i, i + 1) for i in range...  2.45 us
    pallas_call x1, Pallas kernels, per_device(): pl.pallas_call(embed_kernel, out_shape=jax.ShapeDtypeStruct((rows_count,...  2.13 us
    slice x1, local copies, waits for them, and re-layouts, per_device(): frames[count_frames - 2:]  1.18 us
  transfers between devices with their start and end apart: 1, of which 0 were waited for; matrix products, arithmetic and copies ran while one was open for 0% of the time, Pallas kernels for 23%

profile of v2, /device:TPU:0, one launch (start us, length us, event | category | flops | bytes accessed | tf_op | source)
XLA Modules:
  0.0 38.9 jit_solution(8213043716679417273)
XLA Ops:
  0.0 1.2 %slice.3 = bf16[2,48,4096]{2,1,0:T(8,128)(2,1)S(1)} slice(bf16[8,48,4096]{2,1,0:T(8,128)(2,1)} %param.9), slice={[6:8], [0:48], [0:4096]} | slice | bytes 1572864 | tf_op jit(solution)/shard_map/slice | solution.py:233
  1.2 2.4 %collective-permute-start = (bf16[2,48,4096]{2,1,0:T(8,128)(2,1)S(1)}, bf16[2,48,4096]{2,1,0:T(8,128)(2,1)S(1)}, u32[]{:S(2)}, u32[]{:S(2)}) collective-permute-start(bf16[2,48,4096]{2,1,0:T(8,128)(2,1)S(1)} %slice.3), channel_id=1, source_target_pairs={{0,1},{1,2},{2,3},{3,4},{4,5},{5,6},{6,7},{7,8},{8,9},{9,10},{10,1... | collective-permute-start | bytes 2359304 | tf_op jit(solution)/shard_map/ppermute | solution.py:233
  3.6 0.0 copy-start
  3.7 1.9 %copy-done = bf16[8,48,4096]{2,1,0:T(8,128)(2,1)S(1)} copy-done((bf16[8,48,4096]{2,1,0:T(8,128)(2,1)S(1)}, bf16[8,48,4096]{2,1,0:T(8,128)(2,1)}, u32[]{:S(2)}) %copy-start) | copy-done | bytes 3145752
  5.5 0.0 copy-start.2
  5.5 0.9 %copy-done.2 = bf16[16,4096]{1,0:T(8,128)(2,1)S(1)} copy-done((bf16[16,4096]{1,0:T(8,128)(2,1)S(1)}, bf16[16,4096]{1,0:T(8,128)(2,1)}, u32[]{:S(2)}) %copy-start.2) | copy-done | bytes 131096
  6.4 0.0 copy-start.5
  6.4 0.7 %copy-done.5 = f32[128]{0:T(128)S(1)} copy-done((f32[128]{0:T(128)S(1)}, f32[128]{0:T(128)}, u32[]{:S(2)}) %copy-start.5) | copy-done | bytes 536
  7.1 1.6 %copy-done.6 = bf16[512,2048]{1,0:T(8,128)(2,1)S(1)} copy-done((bf16[512,2048]{1,0:T(8,128)(2,1)S(1)}, bf16[512,2048]{1,0:T(8,128)(2,1)}, u32[]{:S(2)}) %copy-start.6) | copy-done | bytes 2097176
  8.7 0.0 copy-start.7
  8.7 0.9 %copy-done.7 = bf16[3,128,128]{2,1,0:T(8,128)(2,1)S(1)} copy-done((bf16[3,128,128]{2,1,0:T(8,128)(2,1)S(1)}, bf16[3,128,128]{2,1,0:T(8,128)(2,1)}, u32[]{:S(2)}) %copy-start.7) | copy-done | bytes 98328
  9.6 0.0 copy-start.8
  9.6 0.7 %copy-done.8 = bf16[128,48]{0,1:T(8,128)(2,1)S(1)} copy-done((bf16[128,48]{0,1:T(8,128)(2,1)S(1)}, bf16[128,48]{0,1:T(8,128)(2,1)}, u32[]{:S(2)}) %copy-start.8) | copy-done | bytes 12312
  10.3 0.0 copy-start.9
  10.3 0.7 %copy-done.9 = s32[4]{0:T(128)S(1)} copy-done((s32[4]{0:T(128)S(1)}, s32[4]{0:T(128)}, u32[]{:S(2)}) %copy-start.9) | copy-done | bytes 40
  10.9 0.0 copy-start.1
  11.0 8.8 %rest.1 = (f32[16,256]{1,0:T(8,128)S(1)}, bf16[512,2048]{1,0:T(8,128)(2,1)S(1)}, bf16[256,192]{1,0:T(8,128)(2,1)S(1)}) custom-call(s32[1]{0:T(128)} %bitcast.4.slab_ref, s32[4]{0:T(128)S(1)} %copy-done.9, bf16[384,4096]{1,0:T(8,128)(2,1)S(1)} %bitcast.8, bf16[48,128]{1,0:T(8,128)(2,1)S(1)} %bitcast.15, bf16[3,128,128]{2,1,0:T(8,128)(2,1)S(1)} %copy-done.7, ...), custom_call_target="tpu_custom_call" | custom-call | flops 4429185024 | bytes 10485760 | tf_op jit(solution)/shard_map/rest/pallas_call | solution.py:241
  19.8 0.0 collective-permute-done
  19.8 0.0 copy-done.1
  19.8 0.0 copy-done.3
  19.8 0.0 copy-done.4
  19.8 3.2 %first.1 = bf16[128,128]{1,0:T(8,128)(2,1)S(1)} custom-call(bf16[96,4096]{1,0:T(8,128)(2,1)S(1)} %bitcast.10, bf16[384,4096]{1,0:T(8,128)(2,1)S(1)} %bitcast.9, s32[1,64]{1,0:T(1,128)S(1)} %bitcast.12, f32[1,128]{1,0:T(1,128)S(1)} %bitcast.14, bf16[16,4096]{1,0:T(8,128)(2,1)S(1)} %copy-done.3, f32[16,256]{1,0:T(8,128)S(1)} %get-tuple-element.8.total_ref, ...), custom_call_target="tpu_custom_call" | custom-call | tf_op jit(solution)/shard_map/first/pallas_call | solution.py:269
  23.1 13.7 %all_to_all.5 = bf16[16,8,128]{2,1,0:T(8,128)(2,1)} all-to-all(bf16[16,8,128]{2,1,0:T(8,128)(2,1)S(1)} %bitcast.11), channel_id=1, replica_groups=mesh['grp'=2,'tok'=16] {'tok'}, dimensions={0} | all-to-all | bytes 65536 | tf_op jit(solution)/shard_map/all_to_all | solution.py:287
  36.8 2.1 %embed.1 = bf16[64,2048]{1,0:T(8,128)(2,1)} custom-call(bf16[128,128]{1,0:T(8,128)(2,1)} %bitcast.16, bf16[64,2048]{1,0:T(8,128)(2,1)} %weight_ref.1), custom_call_target="tpu_custom_call" | custom-call | tf_op jit(solution)/shard_map/embed/pallas_call | solution.py:290
  (3 shorter events, 0.0 us)
Async XLA Ops:
  1.2 18.6 %collective-permute-start = (bf16[2,48,4096]{2,1,0:T(8,128)(2,1)S(1)}, bf16[2,48,4096]{2,1,0:T(8,128)(2,1)S(1)}, u32[]{:S(2)}, u32[]{:S(2)}) collective-permute-start(bf16[2,48,4096]{2,1,0:T(8,128)(2,1)S(1)} %slice.3), channel_id=1, source_target_pairs={{0,1},{1,2},{2,3},{3,4},{4,5},{5,6},{6,7},{7,8},{8,9},{9,10},{10,1... | collective-permute-start | bytes 2359304 | tf_op jit(solution)/shard_map/ppermute | solution.py:233
  3.6 1.9 %copy-start = (bf16[8,48,4096]{2,1,0:T(8,128)(2,1)S(1)}, bf16[8,48,4096]{2,1,0:T(8,128)(2,1)}, u32[]{:S(2)}) copy-start(bf16[8,48,4096]{2,1,0:T(8,128)(2,1)} %param.9) | copy-start | bytes 9437188
  5.5 0.9 %copy-start.2 = (bf16[16,4096]{1,0:T(8,128)(2,1)S(1)}, bf16[16,4096]{1,0:T(8,128)(2,1)}, u32[]{:S(2)}) copy-start(bf16[16,4096]{1,0:T(8,128)(2,1)} %latent_ref.3) | copy-start | bytes 393220
  6.4 0.7 %copy-start.5 = (f32[128]{0:T(128)S(1)}, f32[128]{0:T(128)}, u32[]{:S(2)}) copy-start(f32[128]{0:T(128)} %param.14) | copy-start | bytes 1540
  7.1 1.6 %copy-start.6 = (bf16[512,2048]{1,0:T(8,128)(2,1)S(1)}, bf16[512,2048]{1,0:T(8,128)(2,1)}, u32[]{:S(2)}) copy-start(bf16[512,2048]{1,0:T(8,128)(2,1)} %mid_ref.1) | copy-start | bytes 6291460
  8.7 0.9 %copy-start.7 = (bf16[3,128,128]{2,1,0:T(8,128)(2,1)S(1)}, bf16[3,128,128]{2,1,0:T(8,128)(2,1)}, u32[]{:S(2)}) copy-start(bf16[3,128,128]{2,1,0:T(8,128)(2,1)} %time_ref.1) | copy-start | bytes 294916
  9.6 0.7 %copy-start.8 = (bf16[128,48]{0,1:T(8,128)(2,1)S(1)}, bf16[128,48]{0,1:T(8,128)(2,1)}, u32[]{:S(2)}) copy-start(bf16[128,48]{0,1:T(8,128)(2,1)} %param.12) | copy-start | bytes 36868
  10.3 0.7 %copy-start.9 = (s32[4]{0:T(128)S(1)}, s32[4]{0:T(128)}, u32[]{:S(2)}) copy-start(s32[4]{0:T(128)} %clip_ref.1) | copy-start | bytes 52
  10.9 8.9 %copy-start.1 = (bf16[8,48,4096]{2,1,0:T(8,128)(2,1)S(1)}, bf16[8,48,4096]{2,1,0:T(8,128)(2,1)}, u32[]{:S(2)}) copy-start(bf16[8,48,4096]{2,1,0:T(8,128)(2,1)} %param.9) | copy-start | bytes 9437188
  10.9 8.9 %copy-start.3 = (bf16[16,4096]{1,0:T(8,128)(2,1)S(1)}, bf16[16,4096]{1,0:T(8,128)(2,1)}, u32[]{:S(2)}) copy-start(bf16[16,4096]{1,0:T(8,128)(2,1)} %latent_ref.3) | copy-start | bytes 393220
  11.0 8.9 %copy-start.4 = (s32[64]{0:T(128)S(1)}, s32[64]{0:T(128)}, u32[]{:S(2)}) copy-start(s32[64]{0:T(128)} %param.11) | copy-start | bytes 772

commit v3 on v2

--- a/solution.py
+++ b/solution.py
@@ -60,7 +60,7 @@
 def permuted(mid_ref, midp, patches, block):
     width = block * patches
     i0, i1 = iota((width, width), 0), iota((width, width), 1)
-    permute = (i0 == (i1 % block) * patches + i1 // block).astype(BF16)
+    permute = jnp.where(i0 == (i1 % block) * patches + i1 // block, 0.5, 0.0).astype(BF16)
     for b in range(mid_ref.shape[1] // width):
         at = slice(b * width, (b + 1) * width)
         midp[:, at] = dot(mid_ref[:, at], permute).astype(BF16)
@@ -75,26 +75,35 @@
     )
 
 
-def activate(mixed, gain, regrouped, ab, patches, block):
-    channels = gain.shape[0]
-    cells = mixed.shape[1]
-    for half in range(2):
-        h = mixed[half * channels : (half + 1) * channels]
-        meansq = jnp.sum(h * h, axis=0, keepdims=True) * (1.0 / channels)
-        v = h * lax.rsqrt(meansq + 1e-06) * gain
-        u = (v * jnp.tanh(v) + v).astype(BF16)
-        for b in range(channels // block):
-            row = (b * patches + ab) * block
-            regrouped[row : row + block, half * cells : (half + 1) * cells] = u[
-                b * block : (b + 1) * block
-            ]
+def activate(weights, window, gain, half, regrouped, shape):
+    channels, patches, block = shape
+    lanes = window(0, half).shape[1]
+    for j in range(0, patches, 2):
+        data = jnp.concatenate([window(j, half), window(j + 1, half)], axis=1)
+        mixed = dot(weights, data)
+        sides = []
+        for f in range(2):
+            h = mixed[f * channels : (f + 1) * channels]
+            meansq = jnp.sum(h * h, axis=0, keepdims=True) * (1.0 / channels)
+            v = h * lax.rsqrt(meansq + 1e-06) * gain
+            sides.append((v * jnp.tanh(v) + v).astype(BF16))
+        for a in range(2):
+            at = slice(a * lanes, (a + 1) * lanes)
+            u = jnp.concatenate([side[:, at] for side in sides], axis=1)
+            for b in range(channels // block):
+                row = (b * patches + j + a) * block
+                regrouped[row : row + block, :] = u[b * block : (b + 1) * block, :]
 
 
 def deepen(midp, regrouped, taps):
-    g = dot(midp[...], regrouped[...]) * 0.5
-    m = (g * jnp.tanh(g) + g).astype(BF16)
-    deep, cells = m.shape[0], m.shape[1] // 2
-    return dot(taps[0], m[:, :cells]) + dot(taps[1], m[:, cells:])
+    rows = midp.shape[0] // 2
+    parts = []
+    for at in range(2):
+        g = dot(midp[at * rows : (at + 1) * rows], regrouped[...])
+        parts.append((g * jnp.tanh(g) + g).astype(BF16))
+    both = dot(taps, jnp.concatenate(parts, axis=0))
+    rows, lanes = both.shape[0] // 2, both.shape[1] // 2
+    return both[:rows, :lanes] + both[rows:, lanes:]
 
 
 def clip_state(clip_ref, slab, count_frames, clips):
@@ -112,14 +121,14 @@
     return live, first
 
 
-def routed(latent, slots_ref, ndev, capacity, side):
-    channels, cells = latent.shape
+def routing(slots_ref, ndev, capacity, side, channels):
     rows = slots_ref.shape[1]
+    cells = side * side
     half = side // 2
     slots = slots_ref[...].astype(F32)
     target_row = jnp.floor(slots / rows)
     i0, i1 = iota((rows, rows), 0), iota((rows, rows), 1)
-    slot_col = jnp.sum(jnp.where(i0 == i1, jnp.broadcast_to(slots, (rows, rows)), 0.0), axis=1, keepdims=True)
+    slot_col = column_of(slots)
     target_col = jnp.floor(slot_col / rows)
     place_col = slot_col - target_col * rows
     same = jnp.logical_and(target_col == target_row, i1 < i0)
@@ -130,74 +139,117 @@
     mine = row_of_cell == iota((rows, cells), 0)
     send = jnp.sum(jnp.where(mine, send_col, 0.0), axis=0, keepdims=True)
     place = jnp.sum(jnp.where(mine, place_col, 0.0), axis=0, keepdims=True)
-    lanes = 128
     pick = (iota((ndev * capacity, cells), 0).astype(F32) == send).astype(BF16)
-    feature, cell = iota((lanes, cells), 0), iota((lanes, cells), 1)
+    feature, cell = iota((128, cells), 0), iota((128, cells), 1)
     sub = (cell // side) % 2 * 2 + cell % 2
-    spread = (iota((lanes, channels), 0) // 4 == iota((lanes, channels), 1)).astype(BF16)
-    values = dot(spread, latent)
-    values = jnp.where(feature % 4 == sub, values, 0.0)
     tags = jnp.where(jnp.logical_and(feature == 4 * channels, sub == 0), place + 1.0, 0.0)
-    values = (values + tags).astype(BF16)
+    return pick, tags
+
+
+def routed(latent, pick, tags, side):
+    channels, cells = latent.shape
+    feature, cell = iota((128, cells), 0), iota((128, cells), 1)
+    sub = (cell // side) % 2 * 2 + cell % 2
+    spread = (iota((128, channels), 0) // 4 == iota((128, channels), 1)).astype(BF16)
+    values = (jnp.where(feature % 4 == sub, dot(spread, latent), 0.0) + tags).astype(BF16)
     return lax.dot_general(pick, values, (((1,), (1,)), ((), ())), preferred_element_type=F32).astype(BF16)
 
 
+def frame_taps(latent_ref, pair, deep):
+    at = 2 * pair * deep
+    return jnp.concatenate(
+        [latent_ref[:, at : at + deep], latent_ref[:, at + deep : at + 2 * deep]], axis=0
+    )
+
+
 def rest_kernel(
-    clips, slab_ref, clip_ref, frames_ref, stem_ref, time_ref, gain_ref, mid_ref, latent_ref,
-    total_ref, midp, wfirst_ref, wmask, regrouped,
+    ndev, capacity, side, clips, slab_ref, clip_ref, slots_hbm, frames_hbm, stem_hbm, time_hbm, gain_hbm, mid_hbm, latent_hbm,
+    total_ref, midp, wfirst_ref, pick_ref, tags_ref, slots_ref, stem_ref, time_ref, gain_ref, frames_ref, mid_ref, latent_ref,
+    even, odd, sems,
 ):
-    cin = stem_ref.shape[0]
+    cin, channels = stem_ref.shape
     count_frames = frames_ref.shape[0] // cin
     deep = mid_ref.shape[0]
-    channels = stem_ref.shape[1]
     patches = mid_ref.shape[1] // channels
     cells = frames_ref.shape[1] // patches
-    pairs = count_frames // 2
+    lanes = cells // 2
     block = 16
+    window = 4 * cin
+    moves = [
+        (slots_hbm, slots_ref),
+        (stem_hbm, stem_ref),
+        (time_hbm, time_ref),
+        (gain_hbm, gain_ref),
+        (frames_hbm.at[0:window], frames_ref.at[0:window]),
+        (mid_hbm, mid_ref),
+        (frames_hbm.at[window:], frames_ref.at[window:]),
+        (latent_hbm, latent_ref),
+    ]
+    copies = [pltpu.make_async_copy(a, b, sems.at[i]) for i, (a, b) in enumerate(moves)]
+    for copy in copies:
+        copy.start()
     live, first = clip_state(clip_ref, slab_ref[0], count_frames, clips)
+    for copy in copies[:4]:
+        copy.wait()
+    pick_ref[...], tags_ref[...] = routing(slots_ref, ndev, capacity, side, latent_ref.shape[0])
     band = band_weights(stem_ref, time_ref)
+    gain = column_of(gain_ref[...]) * 0.5
     wfirst_ref[...] = masked(band, first, live, 0, cin)
-    for p in range(1, pairs):
-        wmask[p - 1] = masked(band, first, live, p, cin)
+    for copy in copies[4:]:
+        copy.wait()
     permuted(mid_ref, midp, patches, block)
-    gain = column_of(gain_ref[...]) * 0.5
-    total_ref[...] = jnp.zeros_like(total_ref)
-
-    def pair(p, carry):
-        start = pl.multiple_of((p - 1) * 2 * cin, 2 * cin)
-        for ab in range(patches):
-            mixed = dot(wmask[p - 1], frames_ref[pl.ds(start, 4 * cin), ab * cells : (ab + 1) * cells])
-            activate(mixed, gain, regrouped, ab, patches, block)
-        taps = [
-            latent_ref[:, pl.ds(pl.multiple_of((2 * p + half) * deep, deep), deep)]
-            for half in range(2)
-        ]
-        total_ref[...] += deepen(midp, regrouped, taps)
-        return carry
-
-    lax.fori_loop(1, pairs, pair, 0)
+    units = [(p, half) for p in range(1, count_frames // 2) for half in range(2)]
+    buffers = [even, odd]
+    sums = [None, None]
+
+    def work(q):
+        p, half = units[q]
+        start = (p - 1) * 2 * cin
+
+        def at(ab, half):
+            low = ab * cells + half * lanes
+            return frames_ref[start : start + window, low : low + lanes]
+
+        activate(masked(band, first, live, p, cin), at, gain, half, buffers[q % 2], (channels, patches, block))
+
+    def finish(q):
+        p, half = units[q]
+        part = deepen(midp, buffers[q % 2], frame_taps(latent_ref, p, deep))
+        sums[half] = part if sums[half] is None else sums[half] + part
+
+    work(0)
+    for q in range(1, len(units)):
+        work(q)
+        finish(q - 1)
+    finish(len(units) - 1)
+    total_ref[...] = jnp.concatenate(sums, axis=1)
 
 
 def first_kernel(
-    ndev, capacity, side, prior_ref, frames_ref, slots_ref, gain_ref, latent_ref, total_ref, midp,
-    wfirst_ref, out_ref, regrouped,
+    side, prior_ref, frames_ref, gain_ref, latent_ref, total_ref, midp, wfirst_ref, pick_ref, tags_ref,
+    out_ref, even, odd,
 ):
     channels = gain_ref.shape[1]
     deep = midp.shape[0]
     patches = midp.shape[1] // channels
     cells = prior_ref.shape[1] // patches
-    half_rows = prior_ref.shape[0]
+    lanes = cells // 2
+    rows = prior_ref.shape[0]
     gain = column_of(gain_ref[...]) * 0.5
-    for ab in range(patches):
-        at = slice(ab * cells, (ab + 1) * cells)
-        mixed = dot(wfirst_ref[:, :half_rows], prior_ref[:, at]) + dot(
-            wfirst_ref[:, half_rows:], frames_ref[0:half_rows, at]
+
+    def at(ab, half):
+        low = ab * cells + half * lanes
+        return jnp.concatenate(
+            [prior_ref[:, low : low + lanes], frames_ref[0:rows, low : low + lanes]], axis=0
         )
-        activate(mixed, gain, regrouped, ab, patches, 16)
-    latent = total_ref[...] + deepen(
-        midp, regrouped, [latent_ref[:, :deep], latent_ref[:, deep : 2 * deep]]
-    )
-    out_ref[...] = routed(latent.astype(BF16), slots_ref, ndev, capacity, side)
+
+    shape = (channels, patches, 16)
+    taps = frame_taps(latent_ref, 0, deep)
+    activate(wfirst_ref[...], at, gain, 0, even, shape)
+    activate(wfirst_ref[...], at, gain, 1, odd, shape)
+    sums = [deepen(midp, even, taps), deepen(midp, odd, taps)]
+    latent = total_ref[...] + jnp.concatenate(sums, axis=1)
+    out_ref[...] = routed(latent.astype(BF16), pick_ref[...], tags_ref[...], side)
 
 
 def embed_kernel(incoming_ref, weight_ref, out_ref):
@@ -237,19 +289,30 @@
     gain = norm_gain.reshape(1, channels)
     cells = side * side
     flops = 2 * positions * 2 * channels * 4 * cin + 4 * deep * cells * mid_weight.shape[1]
-    regrouped = pltpu.VMEM((mid_weight.shape[1], 2 * cells), BF16)
-    total, midp, wfirst = pl.pallas_call(
-        functools.partial(rest_kernel, clip_lengths.shape[0]),
+    regrouped = pltpu.VMEM((mid_weight.shape[1], cells), BF16)
+    hbm = pl.BlockSpec(memory_space=pltpu.HBM)
+    total, midp, wfirst, pick, tags = pl.pallas_call(
+        functools.partial(rest_kernel, ndev, capacity, side, clip_lengths.shape[0]),
         out_shape=[
             jax.ShapeDtypeStruct((latents, cells), F32),
             jax.ShapeDtypeStruct(mid_weight.shape, BF16),
             jax.ShapeDtypeStruct((2 * channels, 4 * cin), BF16),
+            jax.ShapeDtypeStruct((ndev * capacity, cells), BF16),
+            jax.ShapeDtypeStruct((128, cells), F32),
         ],
-        in_specs=[smem, smem] + [vmem] * 6,
-        out_specs=[vmem] * 3,
+        in_specs=[smem, smem] + [hbm] * 7,
+        out_specs=[vmem] * 5,
         scratch_shapes=[
-            pltpu.VMEM((count_frames // 2 - 1, 2 * channels, 4 * cin), BF16),
+            pltpu.VMEM((1, rows_count), jnp.int32),
+            pltpu.VMEM((cin, channels), BF16),
+            pltpu.VMEM(time_weight.shape, BF16),
+            pltpu.VMEM((1, channels), F32),
+            pltpu.VMEM(stacked.shape, BF16),
+            pltpu.VMEM(mid_weight.shape, BF16),
+            pltpu.VMEM(latent_weight.shape, BF16),
             regrouped,
+            regrouped,
+            pltpu.SemaphoreType.DMA((8,)),
         ],
         compiler_params=pltpu.CompilerParams(vmem_limit_bytes=VMEM_BYTES),
         cost_estimate=pl.CostEstimate(
@@ -258,31 +321,30 @@
         name="rest",
     )(
         slab.astype(jnp.int32).reshape(1),
-        clip_lengths,
-        stacked,
-        stem_weight.T,
-        time_weight,
-        gain,
-        mid_weight,
-        latent_weight,
+        pltpu.with_memory_space_constraint(clip_lengths, pltpu.HBM),
+        *[
+            pltpu.with_memory_space_constraint(x, pltpu.HBM)
+            for x in (sequence_slot_map.reshape(1, rows_count), stacked, stem_weight.T, time_weight, gain, mid_weight, latent_weight)
+        ],
     )
     outgoing = pl.pallas_call(
-        functools.partial(first_kernel, ndev, capacity, side),
+        functools.partial(first_kernel, side),
         out_shape=jax.ShapeDtypeStruct((ndev * capacity, 128), BF16),
-        in_specs=[vmem] * 8,
+        in_specs=[vmem] * 9,
         out_specs=vmem,
-        scratch_shapes=[regrouped],
+        scratch_shapes=[regrouped, regrouped],
         compiler_params=pltpu.CompilerParams(vmem_limit_bytes=VMEM_BYTES),
         name="first",
     )(
         prior.reshape(2 * cin, positions),
         stacked,
-        sequence_slot_map.reshape(1, rows_count),
         gain,
         latent_weight,
         total,
         midp,
         wfirst,
+        pick,
+        tags,
     )
     incoming = lax.all_to_all(
         outgoing.reshape(ndev, capacity, 128), "tok", split_axis=0, concat_axis=0, tiled=True
@@ -292,6 +354,7 @@
         out_shape=jax.ShapeDtypeStruct((rows_count, patch_embed_weight.shape[1]), BF16),
         in_specs=[vmem, vmem],
         out_specs=vmem,
+        compiler_params=pltpu.CompilerParams(vmem_limit_bytes=4 << 20),
         name="embed",
     )(incoming.reshape(ndev * capacity, 128), patch_embed_weight)
 

time: 39.3 us -> 32.6 us (0.83)
  local copies, waits for them, and re-layouts: 8.49 us -> 1.21 us
  Pallas kernels: 14.2 us -> 15 us
    unnamed x20 -> x8, local copies, waits for them, and re-layouts: 7.31 us -> 0.03 us
    pallas_call x2, Pallas kernels: 12.1 us -> 13.8 us  [the longest x1 11.1 us: per_device(): pl.pallas_call(functools.partial(rest_kernel, ndev, capacity, side, clip_...]
    pallas_call x1, Pallas kernels: 2.13 us -> 1.16 us  [per_device(): pl.pallas_call(embed_kernel, out_shape=jax.ShapeDtypeStruct((rows_count,...]
  transfers between devices with their start and end apart: 1 -> 1, of which waited for: 0 -> 0; matrix products, arithmetic and copies ran while one was open for 0% -> 0% of each run, Pallas kernels for 23% -> 34%
where the time goes in v3:
time: 32.6 us; the launch traced here: 32.3 us
  Pallas kernels  15 us (46%)
  blocking collectives  13.6 us (42%)
  starting transfers between devices  2.45 us (8%)
  local copies, waits for them, and re-layouts  1.21 us (4%)
    all_to_all x1, blocking collectives, per_device(): lax.all_to_all(outgoing.reshape(ndev, capacity, 128), 'tok', split_axis=0...  13.6 us
    pallas_call x1, Pallas kernels, per_device(): pl.pallas_call(functools.partial(rest_kernel, ndev, capacity, side, clip_...  11.1 us
    pallas_call x1, Pallas kernels, per_device(): pl.pallas_call(functools.partial(first_kernel, side), out_shape=jax.Shape...  2.72 us
    ppermute x1, starting transfers between devices, per_device(): lax.ppermute(frames[count_frames - 2:], 'tok', [(i, i + 1) for i in range...  2.45 us
    slice x1, local copies, waits for them, and re-layouts, per_device(): frames[count_frames - 2:]  1.18 us
    pallas_call x1, Pallas kernels, per_device(): pl.pallas_call(embed_kernel, out_shape=jax.ShapeDtypeStruct((rows_count,...  1.16 us
  transfers between devices with their start and end apart: 1, of which 0 were waited for; matrix products, arithmetic and copies ran while one was open for 0% of the time, Pallas kernels for 34%

profile of v3, /device:TPU:0, one launch (start us, length us, event | category | flops | bytes accessed | tf_op | source)
XLA Modules:
  0.0 32.3 jit_solution(11815389008776916307)
XLA Ops:
  0.0 1.2 %slice.3 = bf16[2,48,4096]{2,1,0:T(8,128)(2,1)S(1)} slice(bf16[8,48,4096]{2,1,0:T(8,128)(2,1)} %param.9), slice={[6:8], [0:48], [0:4096]} | slice | bytes 1572864 | tf_op jit(solution)/shard_map/slice | solution.py:285
  1.2 2.4 %collective-permute-start = (bf16[2,48,4096]{2,1,0:T(8,128)(2,1)S(1)}, bf16[2,48,4096]{2,1,0:T(8,128)(2,1)S(1)}, u32[]{:S(2)}, u32[]{:S(2)}) collective-permute-start(bf16[2,48,4096]{2,1,0:T(8,128)(2,1)S(1)} %slice.3), channel_id=1, source_target_pairs={{0,1},{1,2},{2,3},{3,4},{4,5},{5,6},{6,7},{7,8},{8,9},{9,10},{10,1... | collective-permute-start | bytes 2359304 | tf_op jit(solution)/shard_map/ppermute | solution.py:285
  3.6 0.0 copy-start
  3.7 0.0 copy-start.2
  3.7 0.0 copy-start.3
  3.7 11.1 %rest.1 = (f32[16,256]{1,0:T(8,128)S(1)}, bf16[512,2048]{1,0:T(8,128)(2,1)S(1)}, bf16[256,192]{1,0:T(8,128)(2,1)S(1)}, bf16[128,256]{1,0:T(8,128)(2,1)S(1)}, f32[128,256]{1,0:T(8,128)S(1)}) custom-call(s32[1]{0:T(128)} %bitcast.3.slab_ref, s32[4]{0:T(128)} %clip_ref.1, s32[1,64]{1,0:T(1,128)} %bitcast.16, bf16[384,4096]{1,0:T(8,128)(2,1)} %bitcast.8, ...), custom_call_target="tpu_custom_call" | custom-call | flops 4429185024 | bytes 10485760 | tf_op jit(solution)/shard_map/rest/pallas_call | solution.py:294
  14.8 0.0 collective-permute-done
  14.8 0.0 copy-done
  14.8 0.0 copy-done.2
  14.8 0.0 copy-done.3
  14.9 0.0 copy-start.1
  14.9 2.7 %first.1 = bf16[128,128]{1,0:T(8,128)(2,1)S(1)} custom-call(bf16[96,4096]{1,0:T(8,128)(2,1)S(1)} %bitcast.10, bf16[384,4096]{1,0:T(8,128)(2,1)S(1)} %bitcast.9, f32[1,128]{1,0:T(1,128)S(1)} %bitcast.14, bf16[16,4096]{1,0:T(8,128)(2,1)S(1)} %copy-done.2, f32[16,256]{1,0:T(8,128)S(1)} %get-tuple-element.10.total_ref, ...), custom_call_target="tpu_custom_call" | custom-call | tf_op jit(solution)/shard_map/first/pallas_call | solution.py:330
  17.6 13.6 %all_to_all.5 = bf16[16,8,128]{2,1,0:T(8,128)(2,1)S(1)} all-to-all(bf16[16,8,128]{2,1,0:T(8,128)(2,1)S(1)} %bitcast.12), channel_id=1, replica_groups=mesh['grp'=2,'tok'=16] {'tok'}, dimensions={0} | all-to-all | bytes 65536 | tf_op jit(solution)/shard_map/all_to_all | solution.py:349
  31.2 0.0 copy-done.1
  31.2 1.2 %embed.1 = bf16[64,2048]{1,0:T(8,128)(2,1)} custom-call(bf16[128,128]{1,0:T(8,128)(2,1)S(1)} %bitcast.11, bf16[64,2048]{1,0:T(8,128)(2,1)S(1)} %copy-done.1), custom_call_target="tpu_custom_call" | custom-call | tf_op jit(solution)/shard_map/embed/pallas_call | solution.py:352
Async XLA Ops:
  1.2 13.6 %collective-permute-start = (bf16[2,48,4096]{2,1,0:T(8,128)(2,1)S(1)}, bf16[2,48,4096]{2,1,0:T(8,128)(2,1)S(1)}, u32[]{:S(2)}, u32[]{:S(2)}) collective-permute-start(bf16[2,48,4096]{2,1,0:T(8,128)(2,1)S(1)} %slice.3), channel_id=1, source_target_pairs={{0,1},{1,2},{2,3},{3,4},{4,5},{5,6},{6,7},{7,8},{8,9},{9,10},{10,1... | collective-permute-start | bytes 2359304 | tf_op jit(solution)/shard_map/ppermute | solution.py:285
  3.6 11.2 %copy-start = (bf16[8,48,4096]{2,1,0:T(8,128)(2,1)S(1)}, bf16[8,48,4096]{2,1,0:T(8,128)(2,1)}, u32[]{:S(2)}) copy-start(bf16[8,48,4096]{2,1,0:T(8,128)(2,1)} %param.9) | copy-start | bytes 9437188
  3.7 11.2 %copy-start.2 = (bf16[16,4096]{1,0:T(8,128)(2,1)S(1)}, bf16[16,4096]{1,0:T(8,128)(2,1)}, u32[]{:S(2)}) copy-start(bf16[16,4096]{1,0:T(8,128)(2,1)} %latent_ref.1) | copy-start | bytes 393220
  3.7 11.2 %copy-start.3 = (f32[128]{0:T(128)S(1)}, f32[128]{0:T(128)}, u32[]{:S(2)}) copy-start(f32[128]{0:T(128)} %param.14) | copy-start | bytes 1540
  14.9 16.3 %copy-start.1 = (bf16[64,2048]{1,0:T(8,128)(2,1)S(1)}, bf16[64,2048]{1,0:T(8,128)(2,1)}, u32[]{:S(2)}) copy-start(bf16[64,2048]{1,0:T(8,128)(2,1)} %weight_ref.1) | copy-start | bytes 786436
